TPU v7x, 32 devices: a whole 2x2x4 slice. The times are simulated.
32 devices in a mesh: rows: 8 (over z, y), cols: 4 (over x, core).
Axes of the slice: x: 2, y: 2, z: 4, core: 2. Of those that a mesh axis runs over, the one named last changes fastest.
Arguments:
- right_leaf: float32 [4, 2048, 128], P(None, 'rows'), may hold values from -6 to 6
- right_mid: float32 [2, 4096, 128], P(None, 'rows'), may hold values from -6 to 6
- right_root: float32 [8192, 128], P('rows'), may hold values from -6 to 6
- inverse_leaf: float32 [4, 2048, 2048], P(None, 'rows', 'cols'), may hold values from -1 to 2, as said below
- inverse_mid: float32 [2, 4096, 4096], P(None, 'rows', 'cols'), may hold values from -1 to 2, as said below
- inverse_root: float32 [8192, 8192], P('rows', 'cols'), may hold values from -1 to 2, as said below
- leaf_to_mid: float32 [4, 4096, 2048], P(None, 'rows', 'cols'), may hold values from -0.125 to 0.125
- leaf_to_root: float32 [4, 8192, 2048], P(None, 'rows', 'cols'), may hold values from -0.125 to 0.125
- mid_to_root: float32 [2, 8192, 4096], P(None, 'rows', 'cols'), may hold values from -0.09375 to 0.09375
- mask_leaf_mid: int32 [4, 32, 16], replicated, may hold values 0 or 1
- mask_leaf_root: int32 [4, 64, 16], replicated, may hold values 0 or 1
- mask_mid_root: int32 [2, 64, 32], replicated, may hold values 0 or 1
Outputs:
- solved_leaf: float32 [4, 2048, 128], P(None, 'rows')
- solved_mid: float32 [2, 4096, 128], P(None, 'rows')
- solved_root: float32 [8192, 128], P('rows')
Inputs may be any that keep to these rules, and one draw needn't show every extreme that they name: `inverse_leaf`: lower triangular, with its diagonal between 0.5 and 2. `inverse_mid`: lower triangular, with its diagonal between 0.5 and 2. `inverse_root`: lower triangular, with its diagonal between 0.5 and 2.
All inputs are finite; a program needn't handle non-finite values.
Results may differ from a plain program's by a relative error of at most 0.00014.
Values sent between devices are 32-bit elements; how exact they have to be, the bound alone decides.
No kernel may reach another device: no remote copies, remote signals or barrier semaphores. Data moves between devices by JAX's collectives and lax.ppermute only.
A program may use at most 128 MiB of HBM per device.

v0:
```python
import jax
import jax.numpy as jnp
from jax import lax
from jax.sharding import PartitionSpec as P

TILE = 128


def product(matrix, vector):
    return jnp.einsum(
        "src,sck->srk",
        matrix,
        vector,
        precision=lax.Precision.HIGHEST,
        preferred_element_type=jnp.float32,
    )


def own_columns(gathered):
    col_width = gathered.shape[1] // lax.axis_size("cols")
    return lax.dynamic_slice_in_dim(gathered, lax.axis_index("cols") * col_width, col_width, 1)


def masked(values, pattern):
    rows_dev = values.shape[1]
    cols_dev = values.shape[2]
    row_ids = lax.axis_index("rows") * rows_dev + lax.iota(jnp.int32, rows_dev)
    col_ids = lax.axis_index("cols") * cols_dev + lax.iota(jnp.int32, cols_dev)
    row_hot = (row_ids[:, None] // TILE == lax.iota(jnp.int32, pattern.shape[1])[None, :]).astype(
        jnp.float32
    )
    col_hot = (col_ids[:, None] // TILE == lax.iota(jnp.int32, pattern.shape[2])[None, :]).astype(
        jnp.float32
    )
    expanded = jnp.einsum("ra,sab,cb->src", row_hot, pattern.astype(jnp.float32), col_hot)
    return values * expanded


def fetch_columns(block):
    gathered = lax.all_gather(block, "rows", axis=1, tiled=True)
    return own_columns(gathered)


def solve_block(residual, inverse, spread_needed):
    partial_value = product(inverse, fetch_columns(residual))
    solved = lax.psum(partial_value, "cols")
    spread = fetch_columns(solved) if spread_needed else solved
    return (solved, spread)


def body(
    right_leaf,
    right_mid,
    right_root,
    inverse_leaf,
    inverse_mid,
    inverse_root,
    leaf_to_mid,
    leaf_to_root,
    mid_to_root,
    mask_leaf_mid,
    mask_leaf_root,
    mask_mid_root,
):
    factor_lm = masked(leaf_to_mid, mask_leaf_mid)
    factor_lr = masked(leaf_to_root, mask_leaf_root)
    factor_mr = masked(mid_to_root, mask_mid_root)
    solved_leaf, leaf_columns = solve_block(right_leaf, inverse_leaf, True)
    mid_terms = product(factor_lm, leaf_columns)
    mid_part = mid_terms.reshape(2, 2, mid_terms.shape[1], mid_terms.shape[2]).sum(axis=1)
    root_part = product(factor_lr, leaf_columns).sum(axis=0)[None]
    mid_summed, root_summed = lax.psum((mid_part, root_part), "cols")
    resid_mid = right_mid - mid_summed
    solved_mid, mid_columns = solve_block(resid_mid, inverse_mid, True)
    root_more = product(factor_mr, mid_columns).sum(axis=0)[None]
    resid_root = right_root[None] - root_summed - lax.psum(root_more, "cols")
    solved_root, unused_spread = solve_block(resid_root, inverse_root[None], False)
    return (solved_leaf, solved_mid, solved_root[0])


def solution(mesh):
    placed = (
        P(None, "rows", None),
        P(None, "rows", None),
        P("rows", None),
        P(None, "rows", "cols"),
        P(None, "rows", "cols"),
        P("rows", "cols"),
        P(None, "rows", "cols"),
        P(None, "rows", "cols"),
        P(None, "rows", "cols"),
        P(),
        P(),
        P(),
    )
    return jax.shard_map(
        body,
        mesh=mesh,
        in_specs=placed,
        out_specs=(P(None, "rows", None), P(None, "rows", None), P("rows", None)),
        check_vma=False,
    )
```

profile of v0, /device:TPU:0, one launch (start us, length us, event | category | flops | bytes accessed | tf_op | source)
XLA Modules:
  0.0 608.7 jit_solution(15092546820964897420)
XLA Ops:
  7.2 2.2 copy.32
  9.5 78.9 %all-gather.6.cloned.1.call-done = f32[4,2048,128]{1,2,0:T(8,128)} async-done(((f32[4,256,128]{1,2,0:T(8,128)}), f32[4,2048,128]{1,2,0:T(8,128)}) %all-gather.6.cloned.1.call-update) | async-done | bytes 4194320 | tf_op jit(solution)/shard_map/all_gather | solution.py:40
  88.4 4.2 convolution_bitcast_fusion.1
  92.7 31.4 %all-reduce.7.cloned.1.call-done = f32[4,256,128]{1,2,0:T(8,128)} async-done(((f32[4,256,128]{1,2,0:T(8,128)}), f32[4,256,128]{1,2,0:T(8,128)}) %all-reduce.7.cloned.1.call-update) | async-done | bytes 524304 | tf_op jit(solution)/shard_map/psum | solution.py:46
  124.4 2.7 fusion.37
  127.1 74.1 %all-gather.8.cloned.1.call-done = f32[4,2048,128]{1,2,0:T(8,128)} async-done(((f32[4,256,128]{1,2,0:T(8,128)}), f32[4,2048,128]{1,2,0:T(8,128)}) %all-gather.8.cloned.1.call-update) | async-done | bytes 4194320 | tf_op jit(solution)/shard_map/all_gather | solution.py:40
  201.2 7.5 %bitcast_reduce_fusion = f32[2,512,128]{2,1,0:T(8,128)S(1)} fusion(f32[4,2048,128]{1,2,0:T(8,128)} %all-gather.8.cloned.1.call-done, s32[]{:T(128)S(6)} %select_n.49, f32[4,512,512]{2,1,0:T(8,128)} %param.18, f32[4,512,512]{2,1,0:T(8,128)} %fusion.37), kind=kOutput, calls=%fused_computation.12 | convolution fusion | flops 1611792384 | bytes 9961476 | tf_op jit(solution)/shard_map/src,sck->srk/dot_general | solution.py:10
  208.7 1.0 copy.34
  210.0 31.2 %all-reduce.9.cloned.1.call-done = f32[2,512,128]{1,2,0:T(8,128)} async-done(((f32[2,512,128]{1,2,0:T(8,128)}), f32[2,512,128]{1,2,0:T(8,128)}) %all-reduce.9.cloned.1.call-update) | async-done | bytes 524304 | tf_op jit(solution)/shard_map/psum | solution.py:72
  241.3 1.9 sub.35
  243.3 74.0 %all-gather.10.cloned.1.call-done = f32[2,4096,128]{1,2,0:T(8,128)} async-done(((f32[2,512,128]{1,2,0:T(8,128)}), f32[2,4096,128]{1,2,0:T(8,128)}) %all-gather.10.cloned.1.call-update) | async-done | bytes 4194320 | tf_op jit(solution)/shard_map/all_gather | solution.py:40
  317.3 7.7 %convolution_bitcast_fusion.2 = f32[2,512,128]{1,2,0:T(8,128)} fusion(f32[2,512,1024]{2,1,0:T(8,128)} %param.16, f32[2,4096,128]{1,2,0:T(8,128)} %all-gather.10.cloned.1.call-done, s32[]{:T(128)S(6)} %select_n.52), kind=kOutput, calls=%fused_computation.10 | convolution fusion | flops 1610612736 | bytes 5767172 | tf_op jit(solution)/shard_map/src,sck->srk/dot_general | solution.py:10
  325.0 31.5 %all-reduce.11.cloned.1.call-done = f32[2,512,128]{1,2,0:T(8,128)} async-done(((f32[2,512,128]{1,2,0:T(8,128)}), f32[2,512,128]{1,2,0:T(8,128)}) %all-reduce.11.cloned.1.call-update) | async-done | bytes 524304 | tf_op jit(solution)/shard_map/psum | solution.py:46
  357.3 1.3 fusion.35
  358.6 4.5 fusion.29
  363.1 8.7 %fusion.6 = f32[1,1024,128]{2,1,0:T(8,128)} fusion(f32[4,1024,512]{2,1,0:T(8,128)S(1)} %bitcast.56, f32[4,1024,512]{2,1,0:T(8,128)S(1)} %fusion.35, f32[4,2048,128]{1,2,0:T(8,128)} %all-gather.8.cloned.1.call-done, s32[]{:T(128)S(6)} %select_n.49), kind=kOutput, calls=%fused_computation.6 | convolution fusion | flops 3223322624 | bytes 18350084 | tf_op jit(solution)/shard_map/src,sck->srk/dot_general | solution.py:10
  371.9 60.3 %all-gather.12.cloned.1.call-done = f32[2,4096,128]{1,2,0:T(8,128)} async-done(((f32[2,512,128]{1,2,0:T(8,128)}), f32[2,4096,128]{1,2,0:T(8,128)}) %all-gather.12.cloned.1.call-update) | async-done | bytes 4194320 | tf_op jit(solution)/shard_map/all_gather | solution.py:40
  432.2 11.2 %fusion.9 = f32[1,1024,128]{2,1,0:T(8,128)} fusion(f32[2,1024,1024]{2,1,0:T(8,128)} %param.20, f32[2,1024,1024]{2,1,0:T(8,128)} %fusion.29, f32[2,4096,128]{1,2,0:T(8,128)} %all-gather.12.cloned.1.call-done, s32[]{:T(128)S(6)} %select_n.52), kind=kOutput, calls=%fused_computation.7 | convolution fusion | flops 3223322624 | bytes 18350084 | tf_op jit(solution)/shard_map/src,sck->srk/dot_general | solution.py:10
  443.5 34.5 %all-reduce.15.cloned.1.call-done = (f32[1,1024,128]{2,1,0:T(8,128)}, f32[1,1024,128]{2,1,0:T(8,128)}) async-done(((f32[1,1024,128]{2,1,0:T(8,128)}, f32[1,1024,128]{2,1,0:T(8,128)}), (f32[1,1024,128]{2,1,0:T(8,128)}, f32[1,1024,128]{2,1,0:T(8,128)})) %all-reduce.15.cloned.1.call-update) | async-done | bytes 1048592 | tf_op jit(solution)/shard_map/psum | solution.py:76
  478.1 2.1 fusion.23
  480.2 74.6 %all-gather.14.cloned.1.call-done = f32[1,8192,128]{2,1,0:T(8,128)} async-done(((f32[1,1024,128]{2,1,0:T(8,128)}), f32[1,8192,128]{2,1,0:T(8,128)}) %all-gather.14.cloned.1.call-update) | async-done | bytes 4194320 | tf_op jit(solution)/shard_map/all_gather | solution.py:40
  554.8 13.4 %convolution_bitcast_fusion = f32[1024,128]{0,1:T(8,128)} fusion(f32[1024,2048]{1,0:T(8,128)} %param.17, f32[1,8192,128]{2,1,0:T(8,128)} %all-gather.14.cloned.1.call-done, s32[]{:T(128)S(6)} %select_n.55), kind=kOutput, calls=%fused_computation.8 | convolution fusion | flops 3221225472 | bytes 9961476 | tf_op jit(solution)/shard_map/src,sck->srk/dot_general | solution.py:10
  570.3 29.6 %all-reduce.13.cloned.1.call-done = f32[1024,128]{0,1:T(8,128)} async-done(((f32[1024,128]{0,1:T(8,128)}), f32[1024,128]{0,1:T(8,128)}) %all-reduce.13.cloned.1.call-update) | async-done | bytes 524304 | tf_op jit(solution)/shard_map/psum | solution.py:46
  599.9 2.0 copy.40
  (56 shorter events, 3.6 us)
Async XLA Ops:
  7.2 81.2 %copy-start = (f32[4,256,512]{2,1,0:T(8,128)S(1)}, f32[4,256,512]{2,1,0:T(8,128)}, u32[]{:S(2)}) copy-start(f32[4,256,512]{2,1,0:T(8,128)} %param.15) | copy-start | bytes 6291460
  7.2 117.0 %copy-start.6 = (s32[4,32,16]{1,2,0:T(8,128)S(1)}, s32[4,32,16]{1,2,0:T(8,128)}, u32[]{:S(2)}) copy-start(s32[4,32,16]{1,2,0:T(8,128)} %param.21) | copy-start | bytes 24580
  7.2 81.2 %all-gather.6.cloned.1.call-start = ((), (), s32[]{:S(2)}) async-start(), calls=%async_computation | async-start | bytes 4718592 | tf_op jit(solution)/shard_map/all_gather | solution.py:40
  9.4 114.7 %all-reduce.7.cloned.1.call-start = ((), (), s32[]{:S(2)}) async-start(), calls=%async_computation.1 | async-start | bytes 1048576 | tf_op jit(solution)/shard_map/psum | solution.py:46
  92.6 108.6 %all-gather.8.cloned.1.call-start = ((), (), s32[]{:S(2)}) async-start(), calls=%async_computation.2 | async-start | bytes 4718592 | tf_op jit(solution)/shard_map/all_gather | solution.py:40
  124.1 117.1 %all-reduce.9.cloned.1.call-start = ((), (), s32[]{:S(2)}) async-start(), calls=%async_computation.3 | async-start | bytes 1048576 | tf_op jit(solution)/shard_map/psum | solution.py:72
  127.1 82.7 %copy-start.4 = (f32[2,512,128]{2,1,0:T(8,128)S(1)}, f32[2,512,128]{2,1,0:T(8,128)}, u32[]{:S(2)}) copy-start(f32[2,512,128]{2,1,0:T(8,128)} %param.13) | copy-start | bytes 1572868
  209.7 107.5 %all-gather.10.cloned.1.call-start = ((), (), s32[]{:S(2)}) async-start(), calls=%async_computation.4 | async-start | bytes 4718592 | tf_op jit(solution)/shard_map/all_gather | solution.py:40
  210.0 146.8 %copy-start.7 = (s32[2,64,32]{1,2,0:T(8,128)S(1)}, s32[2,64,32]{1,2,0:T(8,128)}, u32[]{:S(2)}) copy-start(s32[2,64,32]{1,2,0:T(8,128)} %param.23) | copy-start | bytes 49156
  210.0 146.8 %copy-start.8 = (s32[4,64,16]{1,2,0:T(8,128)S(1)}, s32[4,64,16]{1,2,0:T(8,128)}, u32[]{:S(2)}) copy-start(s32[4,64,16]{1,2,0:T(8,128)} %param.22) | copy-start | bytes 49156
  243.2 113.4 %all-reduce.11.cloned.1.call-start = ((), (), s32[]{:S(2)}) async-start(), calls=%async_computation.5 | async-start | bytes 1048576 | tf_op jit(solution)/shard_map/psum | solution.py:46
  325.0 107.2 %all-gather.12.cloned.1.call-start = ((), (), s32[]{:S(2)}) async-start(), calls=%async_computation.6 | async-start | bytes 4718592 | tf_op jit(solution)/shard_map/all_gather | solution.py:40
  356.6 121.5 %all-reduce.15.cloned.1.call-start = ((), (), s32[]{:S(2)}) async-start(), calls=%async_computation.9 | async-start | bytes 2097152 | tf_op jit(solution)/shard_map/psum | solution.py:76
  357.3 5.8 slice-start
  358.6 4.6 slice-start.1
  371.9 106.2 %copy-start.5 = (f32[1024,128]{1,0:T(8,128)S(1)}, f32[1024,128]{1,0:T(8,128)}, u32[]{:S(2)}) copy-start(f32[1024,128]{1,0:T(8,128)} %param.14) | copy-start | bytes 1572868
  443.5 111.4 %all-gather.14.cloned.1.call-start = ((), (), s32[]{:S(2)}) async-start(), calls=%async_computation.7 | async-start | bytes 4718592 | tf_op jit(solution)/shard_map/all_gather | solution.py:40
  480.2 119.7 %all-reduce.13.cloned.1.call-start = ((), (), s32[]{:S(2)}) async-start(), calls=%async_computation.8 | async-start | bytes 1048576 | tf_op jit(solution)/shard_map/psum | solution.py:46
  480.2 88.1 %copy-start.2 = (f32[4,256,128]{1,2,0:T(8,128)S(1)}, f32[4,256,128]{1,2,0:T(8,128)}, u32[]{:S(2)}) copy-start(f32[4,256,128]{1,2,0:T(8,128)} %all-reduce.7.cloned.1.call-done) | copy-start | bytes 1572868
  480.2 89.1 %copy-start.3 = (f32[2,512,128]{1,2,0:T(8,128)S(1)}, f32[2,512,128]{1,2,0:T(8,128)}, u32[]{:S(2)}) copy-start(f32[2,512,128]{1,2,0:T(8,128)} %all-reduce.11.cloned.1.call-done) | copy-start | bytes 1572868
  554.8 47.1 %copy-start.1 = (f32[4,256,512]{2,1,0:T(8,128)S(1)}, f32[4,256,512]{2,1,0:T(8,128)}, u32[]{:S(2)}) copy-start(f32[4,256,512]{2,1,0:T(8,128)} %param.15) | copy-start | bytes 6291460
Sparse Core Ops, SparseCore 0:
  10.6 77.7 all-gather.5
  92.8 31.3 all-reduce.6
  126.2 75.0 all-gather.7
  209.9 31.3 all-reduce.8
  243.9 73.3 all-gather.9
  325.1 31.4 all-reduce.10
  358.8 73.3 all-gather.11
  443.6 34.4 all-reduce.14
  481.0 73.8 all-gather.13
  568.4 31.4 all-reduce.12
where the time goes:
time: 609 us
  waiting for transfers between devices  520 us (85%)
  matrix products  61.8 us (10%)
  between operations  14.4 us (2%)
  local copies, waits for them, and re-layouts  7.45 us (1%)
    all_gather x5, waiting for transfers between devices, fetch_columns(): gathered = lax.all_gather(block, 'rows', axis=1, tiled=True)  362 us
    psum x3, waiting for transfers between devices, solve_block(): solved = lax.psum(partial_value, 'cols')  92.6 us
    dot_general x6, matrix products, product(): jnp.einsum('src,sck->srk', matrix, vector, precision=lax.Precision.HIGHES...  52.8 us
    psum x1, waiting for transfers between devices, body(): resid_root = right_root[None] - root_summed - lax.psum(root_more, 'cols')  34.5 us
    psum x1, waiting for transfers between devices, body(): mid_summed, root_summed = lax.psum((mid_part, root_part), 'cols')  31.2 us
  transfers between devices with their start and end apart: 10, of which 10 were waited for; matrix products, arithmetic and copies ran while one was open for 3% of the time, Pallas kernels for 0%

commit v1 on v0

--- a/solution.py
+++ b/solution.py
@@ -1,9 +1,18 @@
+import functools
 import jax
 import jax.numpy as jnp
 from jax import lax
 from jax.sharding import PartitionSpec as P
 
 TILE = 128
+
+
+def digits_map(point, peer_axis):
+    mixed_arr = jax.lax.all_gather(point, peer_axis)
+    return jnp.sum(mixed_arr, axis=0)
+
+
+pass_orders_here = functools.partial(digits_map, peer_axis="cols")
 
 
 def product(matrix, vector):
@@ -43,7 +52,7 @@
 
 def solve_block(residual, inverse, spread_needed):
     partial_value = product(inverse, fetch_columns(residual))
-    solved = lax.psum(partial_value, "cols")
+    solved = pass_orders_here(partial_value)
     spread = fetch_columns(solved) if spread_needed else solved
     return (solved, spread)
 

time: 609 us -> 593 us (0.974); the launches traced: 609 us -> 585 us
  waiting for transfers between devices: 520 us -> 485 us
  other arithmetic: 4.05 us -> 12 us
    psum x3 -> x0, waiting for transfers between devices: 92.6 us -> none  [solve_block(): solved = lax.psum(partial_value, 'cols')]
    all_gather x0 -> x3, waiting for transfers between devices: none -> 62.8 us  [digits_map(): mixed_arr = jax.lax.all_gather(point, peer_axis)]
    reduce_sum x0 -> x3, other arithmetic: none -> 7.96 us  [digits_map(): return jnp.sum(mixed_arr, axis=0)]
where the time goes in v1:
time: 593 us; the launch traced here: 585 us
  waiting for transfers between devices  485 us (82%)
  matrix products  62.5 us (11%)
  between operations  14.8 us (2%)
  other arithmetic  12 us (2%)
  local copies, waits for them, and re-layouts  10 us (2%)
    all_gather x5, waiting for transfers between devices, fetch_columns(): gathered = lax.all_gather(block, 'rows', axis=1, tiled=True)  356 us
    all_gather x3, waiting for transfers between devices, digits_map(): mixed_arr = jax.lax.all_gather(point, peer_axis)  62.8 us
    dot_general x6, matrix products, product(): jnp.einsum('src,sck->srk', matrix, vector, precision=lax.Precision.HIGHES...  53.5 us
    psum x1, waiting for transfers between devices, body(): resid_root = right_root[None] - root_summed - lax.psum(root_more, 'cols')  34.5 us
    psum x1, waiting for transfers between devices, body(): mid_summed, root_summed = lax.psum((mid_part, root_part), 'cols')  31.3 us
  transfers between devices with their start and end apart: 10, of which 10 were waited for; matrix products, arithmetic and copies ran while one was open for 3% of the time, Pallas kernels for 0%

profile of v1, /device:TPU:0, one launch (start us, length us, event | category | flops | bytes accessed | tf_op | source)
XLA Modules:
  0.0 585.2 jit_solution(12179802856103665473)
XLA Ops:
  7.2 2.2 copy.29
  9.5 78.9 %all-gather.12.cloned.1.call-done = f32[4,2048,128]{1,2,0:T(8,128)} async-done(((f32[4,256,128]{1,2,0:T(8,128)}), f32[4,2048,128]{1,2,0:T(8,128)}) %all-gather.12.cloned.1.call-update) | async-done | bytes 4194320 | tf_op jit(solution)/shard_map/all_gather | solution.py:49
  88.4 3.4 convolution_bitcast_fusion.1
  92.9 20.9 %all-gather.22.cloned.1.call-done = f32[16,256,128]{2,1,0:T(8,128)} async-done(((f32[4,256,128]{2,1,0:T(8,128)}), f32[16,256,128]{2,1,0:T(8,128)}) %all-gather.22.cloned.1.call-update) | async-done | bytes 2097168 | tf_op jit(solution)/shard_map/all_gather | solution.py:11
  113.7 2.5 reduce_sum.35
  116.6 2.7 fusion.37
  119.3 70.7 %all-gather.14.cloned.1.call-done = f32[4,2048,128]{2,1,0:T(8,128)} async-done(((f32[4,256,128]{2,1,0:T(8,128)}), f32[4,2048,128]{2,1,0:T(8,128)}) %all-gather.14.cloned.1.call-update) | async-done | bytes 4194320 | tf_op jit(solution)/shard_map/all_gather | solution.py:49
  189.9 7.5 %bitcast_reduce_fusion = f32[2,512,128]{2,1,0:T(8,128)S(1)} fusion(f32[4,2048,128]{2,1,0:T(8,128)} %all-gather.14.cloned.1.call-done, s32[]{:T(128)S(6)} %select_n.49, f32[4,512,512]{2,1,0:T(8,128)} %param.18, f32[4,512,512]{2,1,0:T(8,128)} %fusion.37), kind=kOutput, calls=%fused_computation.12 | convolution fusion | flops 1611792384 | bytes 9961476 | tf_op jit(solution)/shard_map/src,sck->srk/dot_general | solution.py:19
  198.7 31.3 %all-reduce.4.cloned.1.call-done = f32[2,512,128]{1,2,0:T(8,128)} async-done(((f32[2,512,128]{1,2,0:T(8,128)}), f32[2,512,128]{1,2,0:T(8,128)}) %all-reduce.4.cloned.1.call-update) | async-done | bytes 524304 | tf_op jit(solution)/shard_map/psum | solution.py:81
  232.1 74.0 %all-gather.16.cloned.1.call-done = f32[2,4096,128]{1,2,0:T(8,128)} async-done(((f32[2,512,128]{1,2,0:T(8,128)}), f32[2,4096,128]{1,2,0:T(8,128)}) %all-gather.16.cloned.1.call-update) | async-done | bytes 4194320 | tf_op jit(solution)/shard_map/all_gather | solution.py:49
  306.1 6.9 %convolution_bitcast_fusion.2 = f32[2,512,128]{1,2,0:T(8,128)S(1)} fusion(f32[2,512,1024]{2,1,0:T(8,128)} %param.16, f32[2,4096,128]{1,2,0:T(8,128)} %all-gather.16.cloned.1.call-done, s32[]{:T(128)S(6)} %select_n.52), kind=kOutput, calls=%fused_computation.10 | convolution fusion | flops 1610612736 | bytes 5767172 | tf_op jit(solution)/shard_map/src,sck->srk/dot_general | solution.py:19
  314.0 21.0 %all-gather.24.cloned.1.call-done = f32[8,512,128]{2,1,0:T(8,128)} async-done(((f32[2,512,128]{2,1,0:T(8,128)}), f32[8,512,128]{2,1,0:T(8,128)}) %all-gather.24.cloned.1.call-update) | async-done | bytes 2097168 | tf_op jit(solution)/shard_map/all_gather | solution.py:11
  335.0 2.5 reduce_sum.37
  339.5 4.5 fusion.29
  344.1 8.8 %fusion.6 = f32[1,1024,128]{2,1,0:T(8,128)} fusion(f32[4,1024,512]{2,1,0:T(8,128)S(1)} %bitcast.60, f32[4,1024,512]{2,1,0:T(8,128)S(1)} %fusion.35, f32[4,2048,128]{2,1,0:T(8,128)} %all-gather.14.cloned.1.call-done, s32[]{:T(128)S(6)} %select_n.49), kind=kOutput, calls=%fused_computation.6 | convolution fusion | flops 3223322624 | bytes 18350084 | tf_op jit(solution)/shard_map/src,sck->srk/dot_general | solution.py:19
  352.9 58.3 %all-gather.18.cloned.1.call-done = f32[2,4096,128]{2,1,0:T(8,128)} async-done(((f32[2,512,128]{2,1,0:T(8,128)}), f32[2,4096,128]{2,1,0:T(8,128)}) %all-gather.18.cloned.1.call-update) | async-done | bytes 4194320 | tf_op jit(solution)/shard_map/all_gather | solution.py:49
  411.2 13.7 %fusion.9 = f32[1,1024,128]{2,1,0:T(8,128)} fusion(f32[2,1024,1024]{2,1,0:T(8,128)} %param.20, f32[2,1024,1024]{2,1,0:T(8,128)} %fusion.29, f32[2,4096,128]{2,1,0:T(8,128)} %all-gather.18.cloned.1.call-done, s32[]{:T(128)S(6)} %select_n.52), kind=kOutput, calls=%fused_computation.7 | convolution fusion | flops 3223322624 | bytes 18350084 | tf_op jit(solution)/shard_map/src,sck->srk/dot_general | solution.py:19
  424.9 34.5 %all-reduce.6.cloned.1.call-done = (f32[1,1024,128]{2,1,0:T(8,128)}, f32[1,1024,128]{2,1,0:T(8,128)}) async-done(((f32[1,1024,128]{2,1,0:T(8,128)}, f32[1,1024,128]{2,1,0:T(8,128)}), (f32[1,1024,128]{2,1,0:T(8,128)}, f32[1,1024,128]{2,1,0:T(8,128)})) %all-reduce.6.cloned.1.call-update) | async-done | bytes 1048592 | tf_op jit(solution)/shard_map/psum | solution.py:85
  459.4 2.1 fusion.23
  461.5 74.6 %all-gather.20.cloned.1.call-done = f32[1,8192,128]{2,1,0:T(8,128)} async-done(((f32[1,1024,128]{2,1,0:T(8,128)}), f32[1,8192,128]{2,1,0:T(8,128)}) %all-gather.20.cloned.1.call-update) | async-done | bytes 4194320 | tf_op jit(solution)/shard_map/all_gather | solution.py:49
  536.1 13.3 %convolution_bitcast_fusion = f32[1024,128]{0,1:T(8,128)} fusion(f32[1024,2048]{1,0:T(8,128)} %param.17, f32[1,8192,128]{2,1,0:T(8,128)} %all-gather.20.cloned.1.call-done, s32[]{:T(128)S(6)} %select_n.55), kind=kOutput, calls=%fused_computation.8 | convolution fusion | flops 3221225472 | bytes 9961476 | tf_op jit(solution)/shard_map/src,sck->srk/dot_general | solution.py:19
  549.5 21.0 %all-gather.26.cloned.1.call-done = f32[4096,128]{0,1:T(8,128)} async-done(((f32[1024,128]{0,1:T(8,128)}), f32[4096,128]{0,1:T(8,128)}) %all-gather.26.cloned.1.call-update) | async-done | bytes 2097168 | tf_op jit(solution)/shard_map/all_gather | solution.py:11
  570.5 3.6 reshape.170
  574.1 2.9 reduce.1
  (56 shorter events, 8.8 us)
Async XLA Ops:
  7.2 81.2 %copy-start = (f32[4,256,512]{2,1,0:T(8,128)S(1)}, f32[4,256,512]{2,1,0:T(8,128)}, u32[]{:S(2)}) copy-start(f32[4,256,512]{2,1,0:T(8,128)} %param.15) | copy-start | bytes 6291460
  7.2 81.2 %all-gather.12.cloned.1.call-start = ((), (), s32[]{:S(2)}) async-start(), calls=%async_computation | async-start | bytes 4718592 | tf_op jit(solution)/shard_map/all_gather | solution.py:49
  9.4 104.3 %all-gather.22.cloned.1.call-start = ((), (), s32[]{:S(2)}) async-start(), calls=%async_computation.6 | async-start | bytes 2621440 | tf_op jit(solution)/shard_map/all_gather | solution.py:11
  9.5 106.9 %copy-start.4 = (s32[4,32,16]{1,2,0:T(8,128)S(1)}, s32[4,32,16]{1,2,0:T(8,128)}, u32[]{:S(2)}) copy-start(s32[4,32,16]{1,2,0:T(8,128)} %param.21) | copy-start | bytes 24580
  92.8 97.1 %all-gather.14.cloned.1.call-start = ((), (), s32[]{:S(2)}) async-start(), calls=%async_computation.1 | async-start | bytes 4718592 | tf_op jit(solution)/shard_map/all_gather | solution.py:49
  116.3 113.7 %all-reduce.4.cloned.1.call-start = ((), (), s32[]{:S(2)}) async-start(), calls=%async_computation.2 | async-start | bytes 1048576 | tf_op jit(solution)/shard_map/psum | solution.py:81
  119.3 79.2 %copy-start.2 = (f32[2,512,128]{2,1,0:T(8,128)S(1)}, f32[2,512,128]{2,1,0:T(8,128)}, u32[]{:S(2)}) copy-start(f32[2,512,128]{2,1,0:T(8,128)} %param.13) | copy-start | bytes 1572868
  198.4 107.6 %all-gather.16.cloned.1.call-start = ((), (), s32[]{:S(2)}) async-start(), calls=%async_computation.3 | async-start | bytes 4718592 | tf_op jit(solution)/shard_map/all_gather | solution.py:49
  232.0 103.0 %all-gather.24.cloned.1.call-start = ((), (), s32[]{:S(2)}) async-start(), calls=%async_computation.7 | async-start | bytes 2621440 | tf_op jit(solution)/shard_map/all_gather | solution.py:11
  232.0 105.7 %copy-start.5 = (s32[2,64,32]{1,2,0:T(8,128)S(1)}, s32[2,64,32]{1,2,0:T(8,128)}, u32[]{:S(2)}) copy-start(s32[2,64,32]{1,2,0:T(8,128)} %param.23) | copy-start | bytes 49156
  232.0 105.8 %copy-start.6 = (s32[4,64,16]{1,2,0:T(8,128)S(1)}, s32[4,64,16]{1,2,0:T(8,128)}, u32[]{:S(2)}) copy-start(s32[4,64,16]{1,2,0:T(8,128)} %param.22) | copy-start | bytes 49156
  314.0 97.2 %all-gather.18.cloned.1.call-start = ((), (), s32[]{:S(2)}) async-start(), calls=%async_computation.4 | async-start | bytes 4718592 | tf_op jit(solution)/shard_map/all_gather | solution.py:49
  337.6 121.8 %all-reduce.6.cloned.1.call-start = ((), (), s32[]{:S(2)}) async-start(), calls=%async_computation.9 | async-start | bytes 2097152 | tf_op jit(solution)/shard_map/psum | solution.py:85
  338.2 5.8 slice-start
  339.5 4.6 slice-start.1
  352.9 106.5 %copy-start.3 = (f32[1024,128]{1,0:T(8,128)S(1)}, f32[1024,128]{1,0:T(8,128)}, u32[]{:S(2)}) copy-start(f32[1024,128]{1,0:T(8,128)} %param.14) | copy-start | bytes 1572868
  424.8 111.3 %all-gather.20.cloned.1.call-start = ((), (), s32[]{:S(2)}) async-start(), calls=%async_computation.5 | async-start | bytes 4718592 | tf_op jit(solution)/shard_map/all_gather | solution.py:49
  461.5 109.0 %all-gather.26.cloned.1.call-start = ((), (), s32[]{:S(2)}) async-start(), calls=%async_computation.8 | async-start | bytes 2621440 | tf_op jit(solution)/shard_map/all_gather | solution.py:11
  549.5 28.5 %copy-start.1 = (f32[4,256,512]{2,1,0:T(8,128)S(1)}, f32[4,256,512]{2,1,0:T(8,128)}, u32[]{:S(2)}) copy-start(f32[4,256,512]{2,1,0:T(8,128)} %param.15) | copy-start | bytes 6291460
Sparse Core Ops, SparseCore 0:
  10.6 77.7 all-gather.11
  93.0 20.7 all-gather.21
  116.5 73.3 all-gather.13
  198.6 31.4 all-reduce.3
  232.6 73.3 all-gather.15
  314.1 20.8 all-gather.23
  337.7 73.3 all-gather.17
  425.0 34.3 all-reduce.5
  462.3 73.8 all-gather.19
  549.6 20.8 all-gather.25
